TPU v7x, 32 devices: a whole 2x2x4 slice. The times are simulated.
32 devices in a mesh: gx: 16 (over z, y, x), gy: 2 (over core).
Axes of the slice: x: 2, y: 2, z: 4, core: 2. Of those that a mesh axis runs over, the one named last changes fastest.
Arguments:
- snapshot: bfloat16 [3, 128, 32, 1024], P(None, 'gx', 'gy'), may hold values from -6 to 6
- basis: bfloat16 [3, 16, 4, 128, 512], P(None, 'gx', 'gy'), may hold values from -3000 to 3000
- taps: bfloat16 [3, 17], replicated, may hold values from 0.099609375 to 1
Outputs:
- new_modes: bfloat16 [3, 16, 4, 128, 512], P(None, 'gx', 'gy')
- new_mode: float32 [3, 16, 4, 128], P(None, 'gx', 'gy')
- factor: float32 [513, 513], replicated
All inputs are finite; a program needn't handle non-finite values.
Results may differ from a plain program's by a relative error of at most 0.0012.
The roundings to bfloat16 on the way count: a program that leaves them out, or rounds other values in their place, can miss the bound.
Values sent between devices are 32-bit elements; how exact they have to be, the bound alone decides.
No kernel may reach another device: no remote copies, remote signals or barrier semaphores. Data moves between devices by JAX's collectives and lax.ppermute only.
A program may use at most 64 MiB of HBM per device.

v0:
```python
import jax
import jax.numpy as jnp
from jax import lax
from jax.experimental import pallas as pl
from jax.experimental.pallas import tpu as pltpu
from jax.sharding import PartitionSpec as P


STRIDE = 8
TILE = 128
PIVOTS = 32
F32 = jnp.float32
BF16 = jnp.bfloat16
HIGHEST = lax.Precision.HIGHEST


def swap(block, axis, step):
    return lax.ppermute(block, axis, [(i, i ^ step) for i in range(lax.axis_size(axis))])


def swap_by_side(block, steps):
    wide = lax.axis_size("gy")
    pairs = [
        (i * wide + j, (i ^ steps[j & 1]) * wide + j) for i in range(lax.axis_size("gx")) for j in range(wide)
    ]
    return lax.ppermute(block, ("gx", "gy"), pairs)


def bit_groups(size):
    groups, bit = [], 1
    while bit < size:
        groups.append((bit, 2 * bit, 3 * bit) if 4 * bit <= size else (bit,))
        bit *= 4 if 4 * bit <= size else 2
    return groups


def contract_rows(a, b, precision=None):
    return lax.dot_general(
        a, b, (((0,), (0,)), ((), ())), precision=precision, preferred_element_type=F32
    )


def contract_lanes(a, b, precision=None):
    return lax.dot_general(
        a, b, (((1,), (1,)), ((), ())), precision=precision, preferred_element_type=F32
    )


def packed_blocks(chunks):
    whole = chunks - chunks // 4
    blocks = [(p, c) for p in range(chunks) for c in range(p, chunks) if p < c or p < whole]
    guests = {i: (whole + i // 3, i % 3) for i in range(3 * (chunks // 4))}
    return blocks, guests


def gram_kernel(side_ref, rows_ref, out_ref):
    blocks, guests = packed_blocks(rows_ref.shape[1] // TILE)
    half, edge = out_ref.shape[0], TILE // 2
    lane = lax.broadcasted_iota(jnp.int32, (edge, TILE), 1)
    for side in range(2):

        @pl.when(side_ref[0] == side)
        def _():
            tops = range(half * side, half * (side + 1), edge)
            panels = {}
            for p in sorted({blocks[top // TILE][0] for top in tops}):
                last = max(blocks[top // TILE][1] for top in tops if blocks[top // TILE][0] == p)
                panels[p] = contract_rows(
                    rows_ref[:, TILE * p : TILE * (p + 1)], rows_ref[:, TILE * p : TILE * (last + 1)]
                )
            for top in tops:
                p, c = blocks[top // TILE]
                low = top % TILE
                value = panels[p][low : low + edge, TILE * (c - p) : TILE * (c - p + 1)]
                if p == c and low and p in guests:
                    guest, quarter = guests[p]
                    if guest not in panels:
                        own = rows_ref[:, TILE * guest : TILE * (guest + 1)]
                        panels[guest] = contract_rows(own, own)
                    part = panels[guest][edge:, :TILE] if quarter == 2 else panels[guest][:edge, :TILE]
                    value = jnp.where(lane < edge, pltpu.roll(part, edge, 1) if quarter else part, value)
                out_ref[top - half * side : top - half * side + edge, :] = value


def half_gram(side, rows):
    count, modes = rows.shape
    height = TILE * len(packed_blocks(modes // TILE)[0]) // 2
    return pl.pallas_call(
        gram_kernel,
        out_shape=jax.ShapeDtypeStruct((height, TILE), F32),
        in_specs=[pl.BlockSpec(memory_space=pltpu.SMEM), pl.BlockSpec(memory_space=pltpu.VMEM)],
        cost_estimate=pl.CostEstimate(
            flops=2 * count * height * TILE, bytes_accessed=4 * height * TILE, transcendentals=0
        ),
        compiler_params=pltpu.CompilerParams(vmem_limit_bytes=4 << 20),
        name="gram",
    )(side.reshape(1), rows)


def weights(taps_ref, direction, lag):
    line = taps_ref[...].astype(F32)[direction : direction + 1, :]
    found = jnp.zeros(lag.shape, F32)
    for tap in range(2 * STRIDE + 1):
        value = jnp.broadcast_to(line[:, tap : tap + 1], (1, lag.shape[1]))
        found = jnp.where(lag == tap, value, found)
    return found


def parted(index, size, bound):
    if size & (size - 1) == 0:
        return index >> (size.bit_length() - 1), index & (size - 1)
    scale = -(-(1 << 16) // size)
    assert all((i * scale) >> 16 == i // size for i in range(bound))
    quotient = (index * scale) >> 16
    return quotient, index - size * quotient


def filter_kernel(taps_hbm, cells_hbm, out_ref, taps_ref, band, cells, arrived, *, cells_x, cells_y):
    taps_copy = pltpu.make_async_copy(taps_hbm, taps_ref, arrived.at[0])
    cells_copy = pltpu.make_async_copy(cells_hbm, cells, arrived.at[1])
    taps_copy.start()
    cells_copy.start()
    depth, points = band.shape
    height = out_ref.shape[0]
    z = lax.broadcasted_iota(jnp.int32, (TILE, points), 0)
    p = lax.broadcasted_iota(jnp.int32, (TILE, points), 1)
    lag = z - STRIDE * p + STRIDE
    taps_copy.wait()
    pattern = weights(taps_ref, 2, jnp.where(lag < 0, lag + depth, lag))
    for block in range(depth // TILE):
        turned = pltpu.roll(pattern, TILE // STRIDE * block, 1) if block else pattern
        band[TILE * block : TILE * (block + 1), :] = turned.astype(BF16)
    count = cells.shape[0]
    per_y = cells_y // STRIDE
    out = lax.broadcasted_iota(jnp.int32, (height, count), 0)
    cell = lax.broadcasted_iota(jnp.int32, (height, count), 1)
    slot, within = parted(out, height // 9, height)
    kind, r = parted(slot, 3, 9)
    comp, q = parted(within, per_y, height // 9)
    rest, y = parted(cell, cells_y, count)
    cell_comp, x = parted(rest, cells_x, count)
    y = y + jnp.where(kind == 1, -cells_y, jnp.where(kind == 2, cells_y, 0))
    weight = weights(taps_ref, 0, x - STRIDE * (r - 1) + STRIDE)
    weight = weight * weights(taps_ref, 1, y - STRIDE * q + STRIDE)
    weight = jnp.where(cell_comp == comp, weight, 0.0)
    cells_copy.wait()
    along_z = jnp.dot(cells[...], band[...], preferred_element_type=F32)
    out_ref[...] = jnp.dot(weight, along_z, precision=HIGHEST, preferred_element_type=F32)


def local_filter(taps, snapshot):
    comps, cells_x, cells_y, cells_z = snapshot.shape
    assert cells_x == STRIDE
    points = cells_z // STRIDE
    height = 9 * padded_rows(comps * cells_y // STRIDE)
    cells = snapshot.reshape(-1, cells_z)
    return pl.pallas_call(
        lambda *refs: filter_kernel(*refs, cells_x=cells_x, cells_y=cells_y),
        out_shape=jax.ShapeDtypeStruct((height, points), F32),
        in_specs=[pl.BlockSpec(memory_space=pltpu.HBM)] * 2,
        scratch_shapes=[
            pltpu.VMEM(taps.shape, BF16),
            pltpu.VMEM((cells_z, points), BF16),
            pltpu.VMEM(cells.shape, BF16),
            pltpu.SemaphoreType.DMA((2,)),
        ],
        cost_estimate=pl.CostEstimate(
            flops=4 * cells.size * points, bytes_accessed=2 * cells.size, transcendentals=0
        ),
        compiler_params=pltpu.CompilerParams(vmem_limit_bytes=4 << 20),
        name="filter",
    )(*(pltpu.with_memory_space_constraint(array, pltpu.HBM) for array in (taps, cells)))


def padded_rows(rows):
    return -(-rows // 8) * 8


def along_slabs_y(parts):
    height = parts.shape[0] // 3
    own, up, down = parts[:height], parts[height : 2 * height], parts[2 * height :]
    count = lax.axis_size("gy")
    if count == 2:
        return own + swap(jnp.where(lax.axis_index("gy") == 1, down, up), "gy", 1)
    pairs = [(i, i + 1) for i in range(count - 1)]
    low = lax.ppermute(up, "gy", pairs)
    return own + low + lax.ppermute(down, "gy", [(j, i) for i, j in pairs])


def cross_kernel(own_ref, low_ref, high_ref, rows_ref, fresh_ref, out_ref):
    lines, points = fresh_ref.shape
    modes = rows_ref.shape[1]
    fresh = (own_ref[...] + low_ref[...] + high_ref[...]).astype(BF16).astype(F32)
    fresh_ref[...] = fresh[:lines, :]
    total = jnp.zeros((8, modes), F32)
    square = jnp.zeros((1, 1), F32)
    for i in range(lines):
        line = fresh[i : i + 1, :]
        square = square + jnp.sum(line * line, axis=1, keepdims=True)
        left = jnp.broadcast_to(line, (8, points)).astype(BF16)
        total = total + jnp.dot(
            left, rows_ref[points * i : points * (i + 1), :], preferred_element_type=F32
        )
    out_ref[...] = jnp.zeros(out_ref.shape, F32)
    for c in range(modes // TILE):
        out_ref[c : c + 1, :] = total[:1, TILE * c : TILE * (c + 1)]
    out_ref[modes // TILE : modes // TILE + 1, :] = jnp.broadcast_to(square, (1, TILE))


def local_cross(own, low, high, rows):
    points = own.shape[1]
    return pl.pallas_call(
        cross_kernel,
        out_shape=(
            jax.ShapeDtypeStruct((rows.shape[0] // points, points), F32),
            jax.ShapeDtypeStruct((padded_rows(rows.shape[1] // TILE + 1), TILE), F32),
        ),
        cost_estimate=pl.CostEstimate(flops=16 * rows.size, bytes_accessed=2 * rows.size, transcendentals=0),
        compiler_params=pltpu.CompilerParams(vmem_limit_bytes=4 << 20),
        name="cross",
    )(own, low, high, rows)


def split(value):
    parts = []
    for _ in range(3):
        parts.append(value.astype(BF16))
        value = value - parts[-1].astype(F32)
    return parts


def left_parts(value):
    a, b, c = split(value)
    return jnp.concatenate([a, a, b, b, a, c])


def right_parts(value):
    a, b, c = split(value)
    return jnp.concatenate([a, b, a, b, c, a])


def factor_blocks(work, scaled, upper, panels, after):
    modes = work.shape[0]
    chunks = modes // TILE
    groups = PIVOTS // 8
    lane = lax.broadcasted_iota(jnp.int32, (8, TILE), 1)
    row = lax.broadcasted_iota(jnp.int32, (8, TILE), 0)
    for p in panels:
        base = p * TILE
        shift = panels[0] * TILE
        scale_blocks = []
        for j in range(TILE // PIVOTS):
            first = PIVOTS * j
            top = base + first
            rows = [
                [work[top + 8 * g : top + 8 * g + 8, TILE * c : TILE * (c + 1)] for c in range(chunks)]
                for g in range(groups)
            ]
            cols = [
                [
                    jnp.broadcast_to(rows[g][p][:, first + k : first + k + 1], (8, TILE))
                    if g >= k // 8
                    else None
                    for g in range(groups)
                ]
                for k in range(PIVOTS)
            ]
            unit = [jnp.where(lane == first + 8 * g + row, 1.0, 0.0).astype(F32) for g in range(groups)]
            inverse = [jnp.zeros((8, TILE), F32) for _ in range(groups)]
            for k in range(PIVOTS):
                own, sub = k // 8, k % 8
                pivot = cols[k][own][sub : sub + 1, :]
                recip = 1.0 / pivot
                inverse[own] = jnp.where(row == sub, recip, inverse[own])
                mult = {g: cols[k][g] * recip for g in range(own, groups)}
                for later in range(k + 1, PIVOTS):
                    factor = cols[k][later // 8][later % 8 : later % 8 + 1, :]
                    for g in range(later // 8, groups):
                        cols[later][g] = cols[later][g] - mult[g] * factor
                mult[own] = jnp.where(row > sub, mult[own], 0.0)
                for c in range(chunks):
                    pivot_row = rows[own][c][sub : sub + 1, :]
                    for g in range(own, groups):
                        rows[g][c] = rows[g][c] - mult[g] * pivot_row
                pivot_row = unit[own][sub : sub + 1, :]
                for g in range(own, groups):
                    unit[g] = unit[g] - mult[g] * pivot_row
            scale = [jnp.sqrt(part) for part in inverse]
            inside = (lane >= first) & (lane < first + PIVOTS)
            for g in range(groups):
                where = slice(top + 8 * g, top + 8 * g + 8)
                line = slice(top - shift + 8 * g, top - shift + 8 * g + 8)
                for c in range(chunks):
                    cut = slice(TILE * c, TILE * (c + 1))
                    if c < p:
                        upper[line, cut] = jnp.zeros((8, TILE), F32)
                    elif c == p:
                        upper[line, cut] = jnp.where(
                            lane >= first + 8 * g + row, rows[g][c] * scale[g], 0.0
                        )
                    else:
                        upper[line, cut] = rows[g][c] * scale[g]
                    if c >= p:
                        scaled[first + 8 * g : first + 8 * g + 8, cut] = rows[g][c] * inverse[g]
                    work[where, cut] = jnp.where(inside, unit[g], rows[g][c]) if c == p else rows[g][c]
                scale_blocks.append(scale[g])
            end = first + PIVOTS
            if end < TILE:
                left = left_parts(jnp.concatenate([rows[g][p] * inverse[g] for g in range(groups)]))
                wide = lax.broadcasted_iota(jnp.int32, (TILE - end, TILE), 1)
                for cuts in ([p], [c for c in range(chunks) if c != p]):
                    right = [work[top : top + PIVOTS, TILE * c : TILE * (c + 1)] for c in cuts]
                    change = contract_rows(left, right_parts(jnp.concatenate(right, axis=1)))
                    for at, c in enumerate(cuts):
                        cut = slice(TILE * c, TILE * (c + 1))
                        old = work[base + end : base + TILE, cut]
                        if c == p:
                            old = jnp.where((wide >= first) & (wide < end), 0.0, old)
                        work[base + end : base + TILE, cut] = old - change[end:, TILE * at : TILE * (at + 1)]
        block_lane = lax.broadcasted_iota(jnp.int32, (TILE, TILE), 1)
        block_row = lax.broadcasted_iota(jnp.int32, (TILE, TILE), 0)
        own = slice(base, base + TILE)
        work[own, own] = jnp.where(block_lane <= block_row, work[own, own], 0.0)
        if p + 1 < chunks:
            left = left_parts(scaled[:, base + TILE :])
            right = right_parts(work[own, :])
        for i in range(p + 1, chunks):
            below = slice(TILE * i, TILE * (i + 1))
            part = left[:, TILE * (i - p - 1) : TILE * (i - p)]
            gram_part = contract_rows(part, right[:, TILE * i :])
            work[below, TILE * i :] = work[below, TILE * i :] - gram_part
            inverse_part = contract_rows(part, right[:, : base + TILE])
            if p:
                work[below, :base] = work[below, :base] - inverse_part[:, :base]
            work[below, own] = -inverse_part[:, base:]
        for g, scale in enumerate(scale_blocks):
            where = slice(base + 8 * g, base + 8 * g + 8)
            for c in range(p + 1):
                cut = slice(TILE * c, TILE * (c + 1))
                work[where, cut] = work[where, cut] * scale
        after(p)


def early_kernel(side_ref, member_ref, beside_ref, mine_ref, other_ref, work, upper, scaled, blocks, *, total):
    modes = work.shape[0]
    chunks = modes // TILE
    half = blocks.shape[0] // 2
    piece = half // 4
    sides = ((mine_ref, side_ref[0], member_ref[0]), (other_ref, 1 - side_ref[0], beside_ref[0]))
    for part_ref, side, member in sides:
        for step in range(4):
            at = pl.multiple_of(half * side + piece * (member ^ step), 8)
            blocks[pl.ds(at, piece), :] = part_ref[piece * step : piece * (step + 1), :] * (1.0 / total)
    places, guests = packed_blocks(chunks)
    for at, (p, c) in enumerate(places):
        work[TILE * p : TILE * (p + 1), TILE * c : TILE * (c + 1)] = blocks[TILE * at : TILE * (at + 1), :]
    edge = TILE // 2
    lane = lax.broadcasted_iota(jnp.int32, (edge, TILE), 1)
    corners = {}
    for p, guest in guests.items():
        at = TILE * places.index((p, p)) + edge
        corners[guest] = blocks[at : at + edge, :]
    for guest in sorted({guest for guest, _ in corners}):
        top, cut = TILE * guest, slice(TILE * guest, TILE * (guest + 1))
        work[top : top + edge, cut] = jnp.where(
            lane < edge, corners[guest, 0], pltpu.roll(corners[guest, 1], edge, 1)
        )
        work[top + edge : top + TILE, cut] = jnp.where(lane < edge, 0.0, pltpu.roll(corners[guest, 2], edge, 1))
    factor_blocks(work, scaled, upper, range(chunks // 2), lambda p: None)


def early_panels(side, member, beside, mine, other, modes, total):
    height = TILE * len(packed_blocks(modes // TILE)[0])
    smem, vmem = (pl.BlockSpec(memory_space=space) for space in (pltpu.SMEM, pltpu.VMEM))
    return pl.pallas_call(
        lambda *refs: early_kernel(*refs, total=total),
        out_shape=(
            jax.ShapeDtypeStruct((modes, modes), F32),
            jax.ShapeDtypeStruct((modes // TILE // 2 * TILE, modes), F32),
        ),
        in_specs=[smem, smem, smem, vmem, vmem],
        scratch_shapes=[pltpu.VMEM((TILE, modes), F32), pltpu.VMEM((height, TILE), F32)],
        cost_estimate=pl.CostEstimate(
            flops=16 * modes**3, bytes_accessed=8 * modes * modes, transcendentals=modes
        ),
        compiler_params=pltpu.CompilerParams(vmem_limit_bytes=8 << 20),
        name="early",
    )(side.reshape(1), member.reshape(1), beside.reshape(1), mine, other)


def late_kernel(
    early_ref, early_upper_ref, rows_ref, inverse_ref, modes_hbm, factor_hbm, scaled, upper, solved, sent
):
    modes = inverse_ref.shape[0]
    chunks = modes // TILE
    above = early_upper_ref.shape[0]
    copies = [pltpu.make_async_copy(early_upper_ref, factor_hbm.at[:above, :modes], sent.at[chunks])]
    copies[0].start()
    inverse_ref[...] = early_ref[...]

    upper[modes - above : modes - above + 1, :] = jnp.zeros((1, modes), F32)

    def solve(p):
        own = slice(TILE * p, TILE * (p + 1))
        if TILE * p >= above:
            end = TILE * (p + 1) + (p == chunks - 1)
            lines = upper.at[TILE * p - above : end - above, :]
            copy = pltpu.make_async_copy(lines, factor_hbm.at[TILE * p : end, :modes], sent.at[chunks + p])
            copy.start()
            copies.append(copy)
        width = TILE * (p + 1)
        known = inverse_ref[own, :width]
        first = known.astype(BF16)
        second = (known - first.astype(F32)).astype(BF16)
        left = rows_ref[:, :width]
        solved[p] = (contract_lanes(left, first) + contract_lanes(left, second)).astype(BF16)
        copy = pltpu.make_async_copy(solved.at[p], modes_hbm.at[:, own], sent.at[p])
        copy.start()
        copies.append(copy)

    for p in range(chunks // 2):
        solve(p)
    factor_blocks(inverse_ref, scaled, upper, range(chunks // 2, chunks), solve)
    for copy in copies:
        copy.wait()


def late_panels(early, early_upper, rows):
    count, modes = rows.shape
    chunks = modes // TILE
    vmem, hbm = (pl.BlockSpec(memory_space=space) for space in (pltpu.VMEM, pltpu.HBM))
    return pl.pallas_call(
        late_kernel,
        out_shape=(
            jax.ShapeDtypeStruct((modes, modes), F32),
            jax.ShapeDtypeStruct((count, modes), BF16),
            jax.ShapeDtypeStruct((modes + 1, modes + 1), F32),
        ),
        out_specs=(vmem, hbm, hbm),
        scratch_shapes=[
            pltpu.VMEM((TILE, modes), F32),
            pltpu.VMEM((modes + 1 - early_upper.shape[0], modes), F32),
            pltpu.VMEM((chunks, count, TILE), BF16),
            pltpu.SemaphoreType.DMA((2 * chunks,)),
        ],
        cost_estimate=pl.CostEstimate(
            flops=16 * modes**3, bytes_accessed=8 * modes * modes, transcendentals=modes
        ),
        compiler_params=pltpu.CompilerParams(vmem_limit_bytes=10 << 20),
        name="late",
    )(early, early_upper, rows)


def finish_kernel(inverse_ref, sums_ref, fresh_ref, rows_ref, _, mode_ref, column_ref, *, total):
    modes = inverse_ref.shape[0]
    chunks = modes // TILE
    sums = sums_ref[...] * (1.0 / total)
    cross = [sums[c : c + 1, :] for c in range(chunks)]
    square = sums[chunks : chunks + 1, :]
    norm = jnp.zeros((1, TILE), F32)
    back = [jnp.zeros((1, TILE), F32)] * chunks
    for p in range(chunks):
        own = slice(TILE * p, TILE * (p + 1))
        known = [inverse_ref[own, TILE * c : TILE * (c + 1)] for c in range(p + 1)]
        column = sum(known[c] * cross[c] for c in range(p + 1))
        column = jnp.broadcast_to(jnp.sum(column, axis=1, keepdims=True), (TILE, TILE))
        column_ref[own, :] = column
        norm = norm + jnp.sum(column * column, axis=0, keepdims=True)
        for c in range(p + 1):
            back[c] = back[c] + jnp.sum(known[c] * column, axis=0, keepdims=True)
    last = jnp.sqrt(square - norm)
    share = jnp.concatenate(back, axis=1)
    first = share.astype(BF16)
    second = (share - first.astype(F32)).astype(BF16)
    both = jnp.concatenate([jnp.broadcast_to(part, (16, modes)) for part in (first, second)])
    points = fresh_ref.shape[1]
    for i in range(fresh_ref.shape[0]):
        left = rows_ref[points * i : points * (i + 1), :]
        covered = contract_lanes(both, left)
        covered = covered[:1, :] + covered[16:17, :]
        mode_ref[:, points * i : points * (i + 1)] = (fresh_ref[i : i + 1, :] - covered) / last
    column_ref[modes : modes + 1, :] = last


def finish(inverse, sums, fresh, rows, factor, total):
    count, modes = rows.shape
    vmem, hbm = (pl.BlockSpec(memory_space=space) for space in (pltpu.VMEM, pltpu.HBM))
    return pl.pallas_call(
        lambda *refs: finish_kernel(*refs, total=total),
        grid=(1,),
        out_shape=(
            jax.ShapeDtypeStruct((1, count), F32),
            jax.ShapeDtypeStruct((modes + 1, modes + 1), F32),
        ),
        in_specs=[vmem, vmem, vmem, vmem, hbm],
        out_specs=(
            pl.BlockSpec((1, count), lambda i: (0, 0)),
            pl.BlockSpec((modes + 1, TILE), lambda i: (0, modes // TILE)),
        ),
        input_output_aliases={4: 1},
        cost_estimate=pl.CostEstimate(
            flops=64 * modes * modes, bytes_accessed=4 * modes * modes, transcendentals=0
        ),
        compiler_params=pltpu.CompilerParams(vmem_limit_bytes=8 << 20),
        name="finish",
    )(inverse, sums, fresh, rows, factor)


def local(snapshot, basis, taps):
    modes = basis.shape[-1]
    rows = basis.reshape(-1, modes)
    total = rows.shape[0] * lax.axis_size("gx") * lax.axis_size("gy")
    side = lax.axis_index("gy") & 1
    place = lax.axis_index("gx")
    inner, group = place & 3, (place >> 2) & 3
    slabs = lax.axis_size("gx")
    near_steps, far_steps, *others = bit_groups(slabs)
    even = side == 0
    member, beside = jnp.where(even, inner, group), jnp.where(even, group, inner)
    ways = (tuple(zip(near_steps, far_steps)), tuple(zip(far_steps, near_steps)))

    parts = local_filter(taps, snapshot)
    side, parts = lax.optimization_barrier((side, parts))
    parts = along_slabs_y(parts)
    away = swap(half_gram(1 - side, rows), "gy", 1)
    half = half_gram(side, rows) + away
    bit = 2
    while bit < lax.axis_size("gy"):
        half = half + swap(half, "gy", bit)
        bit *= 2

    piece = half.shape[0] // 4
    height = parts.shape[0] // 3
    quarters = half.reshape(4, piece, TILE)

    def quarter_of(index):
        return lax.dynamic_index_in_dim(quarters, index, 0, keepdims=False)

    before, own, after = parts[:height], parts[height : 2 * height], parts[2 * height :]
    odd = (inner & 1) == 1
    outer = (inner == 0) | (inner == 3)
    by_one, by_three = jnp.where(odd, before, after), jnp.where(odd, after, before)
    over = jnp.where(inner == 0, before, after)
    wanted = jnp.where((inner == 0) == even, group - 1, group + 1) & 3
    next_group = (group ^ wanted) == 1

    def exchanged(blocks, riders, way):
        return [
            swap_by_side(block if rider is None else jnp.concatenate([block, rider]), steps)
            for block, rider, steps in zip(blocks, riders, way)
        ]

    got = exchanged(
        [quarter_of(member ^ step) for step in (1, 2, 3)],
        (jnp.where(even, by_one, over), None, jnp.where(even, by_three, over)),
        ways[0],
    )
    quarter = sum([block[:piece] for block in got], quarter_of(member))
    one, three = got[0][piece:], got[2][piece:]

    crossed = jnp.where(outer, jnp.where(next_group, one, three), by_three)
    riders = (jnp.where(even, three, by_one), None, jnp.where(even, three, crossed))
    got = exchanged([quarter] * 3, riders, ways[1])
    quarter = sum([block[:piece] for block in got], quarter)
    if slabs == 16:
        last_one, last_three = got[0][piece:], got[2][piece:]
        near = jnp.where(even, one, last_one)
        passed = jnp.where(outer, jnp.where(next_group, last_one, last_three), three)
        far = jnp.where(even, passed, last_three)
    else:
        for steps in others:
            quarter = sum([swap(quarter, "gx", step) for step in steps], quarter)
        forward = [(i, (i + 1) % slabs) for i in range(slabs)]
        near = lax.ppermute(after, "gx", forward)
        far = lax.ppermute(before, "gx", [(j, i) for i, j in forward])

    fresh, cross = local_cross(own, near, far, rows)
    block = jnp.concatenate([quarter, cross])
    gathered = [block] + exchanged([block] * 3, (None,) * 3, ways[0])
    sums = sum([got[piece:] for got in gathered[1:]], block[piece:])
    mine = jnp.concatenate([got[:piece] for got in gathered])
    other = swap(mine, "gy", 1)
    sums = sums + swap_by_side(sums, ways[1][0])
    for steps in others:
        sums = sum([swap(sums, "gx", step) for step in steps], sums)
    bit = 2
    while bit < lax.axis_size("gy"):
        sums = sums + swap(sums, "gy", bit)
        bit *= 2
    hopped = swap_by_side(sums, ways[1][1])
    sums = sums + hopped
    early, early_upper = early_panels(side, member, beside, mine, other, modes, total)
    sums, early = lax.optimization_barrier((sums, early))
    sums = sums + swap(sums, "gy", 1)
    inverse, new_modes, factor = late_panels(early, early_upper, rows)
    new_mode, factor = finish(inverse, sums, fresh, rows, factor, total)
    return (new_modes.reshape(basis.shape), new_mode.reshape(basis.shape[:-1]), factor)


def solution(mesh):
    in_specs = (P(None, "gx", "gy", None), P(None, "gx", "gy", None, None), P())
    out_specs = (P(None, "gx", "gy", None, None), P(None, "gx", "gy", None), P())

    return jax.shard_map(local, mesh=mesh, in_specs=in_specs, out_specs=out_specs, check_vma=False)
```

profile of v0, /device:TPU:0, one launch (start us, length us, event | category | flops | bytes accessed | tf_op | source)
XLA Modules:
  0.0 55.8 jit_solution(4855445790869424655)
XLA Ops:
  0.6 2.1 %filter.1 = f32[72,128]{1,0:T(8,128)S(1)} custom-call(bf16[3,17]{1,0:T(4,128)(2,1)} %refs_0_.1, bf16[384,1024]{1,0:T(8,128)(2,1)} %bitcast.28), custom_call_target="tpu_custom_call" | custom-call | flops 201326592 | bytes 786432 | tf_op jit(solution)/shard_map/filter/pallas_call | solution.py:157
  2.8 0.6 %collective-permute-start = (f32[24,128]{1,0:T(8,128)S(1)}, f32[24,128]{1,0:T(8,128)S(1)}, u32[]{:S(2)}, u32[]{:S(2)}) collective-permute-start(f32[24,128]{1,0:T(8,128)S(1)} %slice_select_fusion), channel_id=1, source_target_pairs={{0,1},{1,0},{2,3},{3,2},{4,5},{5,4},{6,7},{7,6},{8,9},{9,8},{10,11... | collective-permute-start | bytes 36872 | tf_op jit(solution)/shard_map/ppermute | solution.py:18
  3.9 0.6 %gram.2 = f32[576,128]{1,0:T(8,128)S(1)} custom-call(s32[1]{0:T(128)} %bitcast.1.side_ref.refs_0_, bf16[768,512]{1,0:T(8,128)(2,1)S(1)} %bitcast.22), custom_call_target="tpu_custom_call" | custom-call | flops 113246208 | bytes 294912 | tf_op jit(solution)/shard_map/gram/pallas_call | solution.py:88
  4.5 0.9 %collective-permute-done.1 = f32[576,128]{1,0:T(8,128)S(1)} collective-permute-done((f32[576,128]{1,0:T(8,128)S(1)}, f32[576,128]{1,0:T(8,128)S(1)}, u32[]{:S(2)}, u32[]{:S(2)}) %collective-permute-start.1) | collective-permute-done | bytes 294944 | tf_op jit(solution)/shard_map/ppermute | solution.py:18
  5.5 3.6 %collective-permute-start.4 = (f32[152,128]{1,0:T(8,128)S(1)}, f32[152,128]{1,0:T(8,128)S(1)}, u32[]{:S(2)}, u32[]{:S(2)}) collective-permute-start(f32[152,128]{1,0:T(8,128)S(1)} %pad_maximum_fusion.2), channel_id=1, source_target_pairs={{0,6},{1,25},{2,4},{3,27},{4,2},{5,29},{6,0},{7,31},{8,14},{9,17},... | collective-permute-start | bytes 233480 | tf_op jit(solution)/shard_map/ppermute | solution.py:26
  9.8 4.2 %collective-permute-done.3 = f32[144,128]{1,0:T(8,128)S(1)} collective-permute-done((f32[144,128]{1,0:T(8,128)S(1)}, f32[144,128]{1,0:T(8,128)S(1)}, u32[]{:S(2)}, u32[]{:S(2)}) %collective-permute-start.3) | collective-permute-done | bytes 73760 | tf_op jit(solution)/shard_map/ppermute | solution.py:26
  14.1 3.7 %collective-permute-start.6 = (f32[152,128]{1,0:T(8,128)S(1)}, f32[152,128]{1,0:T(8,128)S(1)}, u32[]{:S(2)}, u32[]{:S(2)}) collective-permute-start(f32[152,128]{1,0:T(8,128)S(1)} %get-tuple-element.39), channel_id=1, source_target_pairs={{0,24},{1,7},{2,26},{3,5},{4,28},{5,3},{6,30},{7,1},{8,16},{9,15},... | collective-permute-start | bytes 233480 | tf_op jit(solution)/shard_map/ppermute | solution.py:26
  17.7 0.8 %collective-permute-start.7 = (f32[144,128]{1,0:T(8,128)S(1)}, f32[144,128]{1,0:T(8,128)S(1)}, u32[]{:S(2)}, u32[]{:S(2)}) collective-permute-start(f32[144,128]{1,0:T(8,128)S(1)} %slice_add_fusion.2), channel_id=1, source_target_pairs={{0,16},{1,5},{2,18},{3,7},{4,20},{5,1},{6,22},{7,3},{8,24},{9,13},... | collective-permute-start | bytes 221192 | tf_op jit(solution)/shard_map/ppermute | solution.py:26
  18.5 1.9 %collective-permute-done.6 = f32[152,128]{1,0:T(8,128)S(1)} collective-permute-done((f32[152,128]{1,0:T(8,128)S(1)}, f32[152,128]{1,0:T(8,128)S(1)}, u32[]{:S(2)}, u32[]{:S(2)}) %collective-permute-start.6) | collective-permute-done | bytes 77856 | tf_op jit(solution)/shard_map/ppermute | solution.py:26
  20.4 1.8 %collective-permute-done.5 = f32[152,128]{1,0:T(8,128)S(1)} collective-permute-done((f32[152,128]{1,0:T(8,128)S(1)}, f32[152,128]{1,0:T(8,128)S(1)}, u32[]{:S(2)}, u32[]{:S(2)}) %collective-permute-start.5) | collective-permute-done | bytes 77856 | tf_op jit(solution)/shard_map/ppermute | solution.py:26
  22.4 0.6 %collective-permute-done.7 = f32[144,128]{1,0:T(8,128)S(1)} collective-permute-done((f32[144,128]{1,0:T(8,128)S(1)}, f32[144,128]{1,0:T(8,128)S(1)}, u32[]{:S(2)}, u32[]{:S(2)}) %collective-permute-start.7) | collective-permute-done | bytes 73760 | tf_op jit(solution)/shard_map/ppermute | solution.py:26
  23.0 1.5 %collective-permute-start.10 = (f32[152,128]{1,0:T(8,128)S(1)}, f32[152,128]{1,0:T(8,128)S(1)}, u32[]{:S(2)}, u32[]{:S(2)}) collective-permute-start(f32[152,128]{1,0:T(8,128)S(1)} %pad_maximum_fusion.5), channel_id=1, source_target_pairs={{0,6},{1,25},{2,4},{3,27},{4,2},{5,29},{6,0},{7,31},{8,14},{9,17},... | collective-permute-start | bytes 233480 | tf_op jit(solution)/shard_map/ppermute | solution.py:26
  24.5 1.5 %collective-permute-start.9 = (f32[152,128]{1,0:T(8,128)S(1)}, f32[152,128]{1,0:T(8,128)S(1)}, u32[]{:S(2)}, u32[]{:S(2)}) collective-permute-start(f32[152,128]{1,0:T(8,128)S(1)} %pad_maximum_fusion.5), channel_id=1, source_target_pairs={{0,4},{1,17},{2,6},{3,19},{4,0},{5,21},{6,2},{7,23},{8,12},{9,25},... | collective-permute-start | bytes 233480 | tf_op jit(solution)/shard_map/ppermute | solution.py:26
  26.0 0.5 collective-permute-start.8
  26.6 1.8 %collective-permute-done.10 = f32[152,128]{1,0:T(8,128)S(1)} collective-permute-done((f32[152,128]{1,0:T(8,128)S(1)}, f32[152,128]{1,0:T(8,128)S(1)}, u32[]{:S(2)}, u32[]{:S(2)}) %collective-permute-start.10) | collective-permute-done | bytes 77856 | tf_op jit(solution)/shard_map/ppermute | solution.py:26
  28.4 0.8 %collective-permute-done.9 = f32[152,128]{1,0:T(8,128)S(1)} collective-permute-done((f32[152,128]{1,0:T(8,128)S(1)}, f32[152,128]{1,0:T(8,128)S(1)}, u32[]{:S(2)}, u32[]{:S(2)}) %collective-permute-start.9) | collective-permute-done | bytes 77856 | tf_op jit(solution)/shard_map/ppermute | solution.py:26
  29.2 1.2 %collective-permute-done.8 = f32[152,128]{1,0:T(8,128)S(1)} collective-permute-done((f32[152,128]{1,0:T(8,128)S(1)}, f32[152,128]{1,0:T(8,128)S(1)}, u32[]{:S(2)}, u32[]{:S(2)}) %collective-permute-start.8) | collective-permute-done | bytes 77856 | tf_op jit(solution)/shard_map/ppermute | solution.py:26
  30.6 2.1 %collective-permute-start.11 = (f32[8,128]{1,0:T(8,128)S(1)}, f32[8,128]{1,0:T(8,128)S(1)}, u32[]{:S(2)}, u32[]{:S(2)}) collective-permute-start(f32[8,128]{1,0:T(8,128)S(1)} %slice_add_fusion.5), channel_id=1, source_target_pairs={{0,8},{1,3},{2,10},{3,1},{4,12},{5,7},{6,14},{7,5},{8,0},{9,11},{1... | collective-permute-start | bytes 12296 | tf_op jit(solution)/shard_map/ppermute | solution.py:26
  32.7 1.6 %collective-permute-done.11 = f32[8,128]{1,0:T(8,128)S(1)} collective-permute-done((f32[8,128]{1,0:T(8,128)S(1)}, f32[8,128]{1,0:T(8,128)S(1)}, u32[]{:S(2)}, u32[]{:S(2)}) %collective-permute-start.11) | collective-permute-done | bytes 4128 | tf_op jit(solution)/shard_map/ppermute | solution.py:26
  34.2 1.7 %collective-permute-start.12 = (f32[8,128]{1,0:T(8,128)S(1)}, f32[8,128]{1,0:T(8,128)S(1)}, u32[]{:S(2)}, u32[]{:S(2)}) collective-permute-start(f32[8,128]{1,0:T(8,128)S(1)} %add.75), channel_id=1, source_target_pairs={{0,16},{1,5},{2,18},{3,7},{4,20},{5,1},{6,22},{7,3},{8,24},{9,13},... | collective-permute-start | bytes 12296 | tf_op jit(solution)/shard_map/ppermute | solution.py:26
  35.9 2.8 %collective-permute-done.12 = f32[8,128]{1,0:T(8,128)S(1)} collective-permute-done((f32[8,128]{1,0:T(8,128)S(1)}, f32[8,128]{1,0:T(8,128)S(1)}, u32[]{:S(2)}, u32[]{:S(2)}) %collective-permute-start.12) | collective-permute-done | bytes 4128 | tf_op jit(solution)/shard_map/ppermute | solution.py:26
  38.8 7.3 %early.1 = (f32[512,512]{1,0:T(8,128)S(1)}, f32[256,512]{1,0:T(8,128)S(1)}) custom-call(s32[1]{0:T(128)} %bitcast.1.side_ref.refs_0_, s32[1]{0:T(128)} %bitcast.9.refs_1_, s32[1]{0:T(128)} %bitcast.10.refs_2_, f32[576,128]{1,0:T(8,128)S(1)} %pad_maximum_fusion.refs_3_, f32[576,128]{1,0:T(8,128)S(1)} %collective-permute-done.13.refs_4_), custom_call_target="tpu_custom_call" | custom-call | flops 2147483648 | bytes 2097152 | tf_op jit(solution)/shard_map/early/pallas_call | solution.py:375
  46.2 8.5 %late.1 = (f32[512,512]{1,0:T(8,128)S(1)}, bf16[768,512]{1,0:T(8,128)(2,1)}, f32[513,513]{1,0:T(8,128)}) custom-call(f32[512,512]{1,0:T(8,128)S(1)} %get-tuple-element.20.early_ref, f32[256,512]{1,0:T(8,128)S(1)} %get-tuple-element.21.early_upper_ref, bf16[768,512]{1,0:T(8,128)(2,1)S(1)} %bitcast.24), custom_call_target="tpu_custom_call" | custom-call | flops 2147483648 | bytes 2097152 | tf_op jit(solution)/shard_map/late/pallas_call | solution.py:432
  54.7 1.1 %finish.1 = (f32[1,768]{1,0:T(1,128)}, f32[513,513]{1,0:T(8,128)}) custom-call(f32[512,512]{1,0:T(8,128)S(1)} %get-tuple-element.23.refs_0_, f32[8,128]{1,0:T(8,128)S(1)} %add.77.refs_1_, f32[6,128]{1,0:T(8,128)S(1)} %get-tuple-element.25.refs_2_, bf16[768,512]{1,0:T(8,128)(2,1)S(1)} %bitcast.25, ...), custom_call_target="tpu_custom_call", output_to_operand_aliasing={{1}: (4, {})} | custom-call | flops 16777216 | bytes 1048576 | tf_op jit(solution)/shard_map/finish/pallas_call | solution.py:488
  (36 shorter events, 1.8 us)
Async XLA Ops:
  0.6 2.7 %copy-start = (bf16[3,1,2,128,512]{4,3,2,1,0:T(8,128)(2,1)S(1)}, bf16[3,1,2,128,512]{4,3,2,1,0:T(8,128)(2,1)}, u32[]{:S(2)}) copy-start(bf16[3,1,2,128,512]{4,3,2,1,0:T(8,128)(2,1)} %param.4) | copy-start | bytes 2359300
  2.8 1.7 %collective-permute-start = (f32[24,128]{1,0:T(8,128)S(1)}, f32[24,128]{1,0:T(8,128)S(1)}, u32[]{:S(2)}, u32[]{:S(2)}) collective-permute-start(f32[24,128]{1,0:T(8,128)S(1)} %slice_select_fusion), channel_id=1, source_target_pairs={{0,1},{1,0},{2,3},{3,2},{4,5},{5,4},{6,7},{7,6},{8,9},{9,8},{10,11... | collective-permute-start | bytes 36872 | tf_op jit(solution)/shard_map/ppermute | solution.py:18
  3.8 1.6 %collective-permute-start.1 = (f32[576,128]{1,0:T(8,128)S(1)}, f32[576,128]{1,0:T(8,128)S(1)}, u32[]{:S(2)}, u32[]{:S(2)}) collective-permute-start(f32[576,128]{1,0:T(8,128)S(1)} %gram.3), channel_id=1, source_target_pairs={{0,1},{1,0},{2,3},{3,2},{4,5},{5,4},{6,7},{7,6},{8,9},{9,8},{10,11... | collective-permute-start | bytes 884744 | tf_op jit(solution)/shard_map/ppermute | solution.py:18
  5.5 8.5 %collective-permute-start.4 = (f32[152,128]{1,0:T(8,128)S(1)}, f32[152,128]{1,0:T(8,128)S(1)}, u32[]{:S(2)}, u32[]{:S(2)}) collective-permute-start(f32[152,128]{1,0:T(8,128)S(1)} %pad_maximum_fusion.2), channel_id=1, source_target_pairs={{0,6},{1,25},{2,4},{3,27},{4,2},{5,29},{6,0},{7,31},{8,14},{9,17},... | collective-permute-start | bytes 233480 | tf_op jit(solution)/shard_map/ppermute | solution.py:26
  9.1 4.9 %collective-permute-start.2 = (f32[152,128]{1,0:T(8,128)S(1)}, f32[152,128]{1,0:T(8,128)S(1)}, u32[]{:S(2)}, u32[]{:S(2)}) collective-permute-start(f32[152,128]{1,0:T(8,128)S(1)} %pad_maximum_fusion.1), channel_id=1, source_target_pairs={{0,2},{1,9},{2,0},{3,11},{4,6},{5,13},{6,4},{7,15},{8,10},{9,1},{1... | collective-permute-start | bytes 233480 | tf_op jit(solution)/shard_map/ppermute | solution.py:26
  9.6 4.4 %collective-permute-start.3 = (f32[144,128]{1,0:T(8,128)S(1)}, f32[144,128]{1,0:T(8,128)S(1)}, u32[]{:S(2)}, u32[]{:S(2)}) collective-permute-start(f32[144,128]{1,0:T(8,128)S(1)} %get-tuple-element.34), channel_id=1, source_target_pairs={{0,4},{1,17},{2,6},{3,19},{4,0},{5,21},{6,2},{7,23},{8,12},{9,25},... | collective-permute-start | bytes 221192 | tf_op jit(solution)/shard_map/ppermute | solution.py:26
  14.1 6.3 %collective-permute-start.6 = (f32[152,128]{1,0:T(8,128)S(1)}, f32[152,128]{1,0:T(8,128)S(1)}, u32[]{:S(2)}, u32[]{:S(2)}) collective-permute-start(f32[152,128]{1,0:T(8,128)S(1)} %get-tuple-element.39), channel_id=1, source_target_pairs={{0,24},{1,7},{2,26},{3,5},{4,28},{5,3},{6,30},{7,1},{8,16},{9,15},... | collective-permute-start | bytes 233480 | tf_op jit(solution)/shard_map/ppermute | solution.py:26
  17.7 4.4 %collective-permute-start.5 = (f32[152,128]{1,0:T(8,128)S(1)}, f32[152,128]{1,0:T(8,128)S(1)}, u32[]{:S(2)}, u32[]{:S(2)}) collective-permute-start(f32[152,128]{1,0:T(8,128)S(1)} %get-tuple-element.40), channel_id=1, source_target_pairs={{0,8},{1,3},{2,10},{3,1},{4,12},{5,7},{6,14},{7,5},{8,0},{9,11},{1... | collective-permute-start | bytes 233480 | tf_op jit(solution)/shard_map/ppermute | solution.py:26
  17.7 5.3 %collective-permute-start.7 = (f32[144,128]{1,0:T(8,128)S(1)}, f32[144,128]{1,0:T(8,128)S(1)}, u32[]{:S(2)}, u32[]{:S(2)}) collective-permute-start(f32[144,128]{1,0:T(8,128)S(1)} %slice_add_fusion.2), channel_id=1, source_target_pairs={{0,16},{1,5},{2,18},{3,7},{4,20},{5,1},{6,22},{7,3},{8,24},{9,13},... | collective-permute-start | bytes 221192 | tf_op jit(solution)/shard_map/ppermute | solution.py:26
  23.0 5.4 %collective-permute-start.10 = (f32[152,128]{1,0:T(8,128)S(1)}, f32[152,128]{1,0:T(8,128)S(1)}, u32[]{:S(2)}, u32[]{:S(2)}) collective-permute-start(f32[152,128]{1,0:T(8,128)S(1)} %pad_maximum_fusion.5), channel_id=1, source_target_pairs={{0,6},{1,25},{2,4},{3,27},{4,2},{5,29},{6,0},{7,31},{8,14},{9,17},... | collective-permute-start | bytes 233480 | tf_op jit(solution)/shard_map/ppermute | solution.py:26
  24.5 4.7 %collective-permute-start.9 = (f32[152,128]{1,0:T(8,128)S(1)}, f32[152,128]{1,0:T(8,128)S(1)}, u32[]{:S(2)}, u32[]{:S(2)}) collective-permute-start(f32[152,128]{1,0:T(8,128)S(1)} %pad_maximum_fusion.5), channel_id=1, source_target_pairs={{0,4},{1,17},{2,6},{3,19},{4,0},{5,21},{6,2},{7,23},{8,12},{9,25},... | collective-permute-start | bytes 233480 | tf_op jit(solution)/shard_map/ppermute | solution.py:26
  26.0 4.4 %collective-permute-start.8 = (f32[152,128]{1,0:T(8,128)S(1)}, f32[152,128]{1,0:T(8,128)S(1)}, u32[]{:S(2)}, u32[]{:S(2)}) collective-permute-start(f32[152,128]{1,0:T(8,128)S(1)} %pad_maximum_fusion.5), channel_id=1, source_target_pairs={{0,2},{1,9},{2,0},{3,11},{4,6},{5,13},{6,4},{7,15},{8,10},{9,1},{1... | collective-permute-start | bytes 233480 | tf_op jit(solution)/shard_map/ppermute | solution.py:26
  30.5 8.3 %collective-permute-start.13 = (f32[576,128]{1,0:T(8,128)S(1)}, f32[576,128]{1,0:T(8,128)S(1)}, u32[]{:S(2)}, u32[]{:S(2)}) collective-permute-start(f32[576,128]{1,0:T(8,128)S(1)} %pad_maximum_fusion.refs_3_), channel_id=1, source_target_pairs={{0,1},{1,0},{2,3},{3,2},{4,5},{5,4},{6,7},{7,6},{8,9},{9,8},{10,11... | collective-permute-start | bytes 884744 | tf_op jit(solution)/shard_map/ppermute | solution.py:18
  30.6 3.7 %collective-permute-start.11 = (f32[8,128]{1,0:T(8,128)S(1)}, f32[8,128]{1,0:T(8,128)S(1)}, u32[]{:S(2)}, u32[]{:S(2)}) collective-permute-start(f32[8,128]{1,0:T(8,128)S(1)} %slice_add_fusion.5), channel_id=1, source_target_pairs={{0,8},{1,3},{2,10},{3,1},{4,12},{5,7},{6,14},{7,5},{8,0},{9,11},{1... | collective-permute-start | bytes 12296 | tf_op jit(solution)/shard_map/ppermute | solution.py:26
  34.2 4.5 %collective-permute-start.12 = (f32[8,128]{1,0:T(8,128)S(1)}, f32[8,128]{1,0:T(8,128)S(1)}, u32[]{:S(2)}, u32[]{:S(2)}) collective-permute-start(f32[8,128]{1,0:T(8,128)S(1)} %add.75), channel_id=1, source_target_pairs={{0,16},{1,5},{2,18},{3,7},{4,20},{5,1},{6,22},{7,3},{8,24},{9,13},... | collective-permute-start | bytes 12296 | tf_op jit(solution)/shard_map/ppermute | solution.py:26
  46.1 8.6 %collective-permute-start.14 = (f32[8,128]{1,0:T(8,128)S(1)}, f32[8,128]{1,0:T(8,128)S(1)}, u32[]{:S(2)}, u32[]{:S(2)}) collective-permute-start(f32[8,128]{1,0:T(8,128)S(1)} %add.76), channel_id=1, source_target_pairs={{0,1},{1,0},{2,3},{3,2},{4,5},{5,4},{6,7},{7,6},{8,9},{9,8},{10,11... | collective-permute-start | bytes 12296 | tf_op jit(solution)/shard_map/ppermute | solution.py:18
where the time goes:
time: 55.9 us; the launch traced here: 55.8 us
  Pallas kernels  20.3 us (36%)
  waiting for transfers between devices  17.7 us (32%)
  starting transfers between devices  16.7 us (30%)
  between operations  0.85 us (2%)
    ppermute x11, waiting for transfers between devices, swap_by_side(): return lax.ppermute(block, ('gx', 'gy'), pairs)  16.8 us
    ppermute x11, starting transfers between devices, swap_by_side(): return lax.ppermute(block, ('gx', 'gy'), pairs)  16 us
    pallas_call x1, Pallas kernels, late_panels(): pl.pallas_call(late_kernel, out_shape=(jax.ShapeDtypeStruct((modes, modes...  8.47 us
    pallas_call x1, Pallas kernels, early_panels(): pl.pallas_call(lambda *refs: early_kernel(*refs, total=total), out_shape=...  7.33 us
    pallas_call x1, Pallas kernels, local_filter(): pl.pallas_call(lambda *refs: filter_kernel(*refs, cells_x=cells_x, cells_...  2.1 us
  transfers between devices with their start and end apart: 15, of which 10 were waited for; matrix products, arithmetic and copies ran while one was open for 0% of the time, Pallas kernels for 17%

commit v1 on v0

--- a/solution.py
+++ b/solution.py
@@ -278,12 +278,13 @@
                     for g in range(later // 8, groups):
                         cols[later][g] = cols[later][g] - mult[g] * factor
                 mult[own] = jnp.where(row > sub, mult[own], 0.0)
+                below = range(own + (sub == 7), groups)
                 for c in range(chunks):
                     pivot_row = rows[own][c][sub : sub + 1, :]
-                    for g in range(own, groups):
+                    for g in below:
                         rows[g][c] = rows[g][c] - mult[g] * pivot_row
                 pivot_row = unit[own][sub : sub + 1, :]
-                for g in range(own, groups):
+                for g in below:
                     unit[g] = unit[g] - mult[g] * pivot_row
             scale = [jnp.sqrt(part) for part in inverse]
             inside = (lane >= first) & (lane < first + PIVOTS)

time: 55.9 us -> 55.9 us (level)
  no operation moved by 1% of the time
where the time goes in v1:
time: 55.9 us; the launch traced here: 55.7 us
  Pallas kernels  20.2 us (36%)
  waiting for transfers between devices  17.7 us (32%)
  starting transfers between devices  16.7 us (30%)
  between operations  0.85 us (2%)
    ppermute x11, waiting for transfers between devices, swap_by_side(): return lax.ppermute(block, ('gx', 'gy'), pairs)  16.8 us
    ppermute x11, starting transfers between devices, swap_by_side(): return lax.ppermute(block, ('gx', 'gy'), pairs)  16 us
    pallas_call x1, Pallas kernels, late_panels(): pl.pallas_call(late_kernel, out_shape=(jax.ShapeDtypeStruct((modes, modes...  8.42 us
    pallas_call x1, Pallas kernels, early_panels(): pl.pallas_call(lambda *refs: early_kernel(*refs, total=total), out_shape=...  7.33 us
    pallas_call x1, Pallas kernels, local_filter(): pl.pallas_call(lambda *refs: filter_kernel(*refs, cells_x=cells_x, cells_...  2.1 us
  transfers between devices with their start and end apart: 15, of which 10 were waited for; matrix products, arithmetic and copies ran while one was open for 0% of the time, Pallas kernels for 17%

profile of v1, /device:TPU:0, one launch (start us, length us, event | category | flops | bytes accessed | tf_op | source)
XLA Modules:
  0.0 55.7 jit_solution(3754692780786748553)
XLA Ops:
  0.6 2.1 %filter.1 = f32[72,128]{1,0:T(8,128)S(1)} custom-call(bf16[3,17]{1,0:T(4,128)(2,1)} %refs_0_.1, bf16[384,1024]{1,0:T(8,128)(2,1)} %bitcast.28), custom_call_target="tpu_custom_call" | custom-call | flops 201326592 | bytes 786432 | tf_op jit(solution)/shard_map/filter/pallas_call | solution.py:157
  2.8 0.6 %collective-permute-start = (f32[24,128]{1,0:T(8,128)S(1)}, f32[24,128]{1,0:T(8,128)S(1)}, u32[]{:S(2)}, u32[]{:S(2)}) collective-permute-start(f32[24,128]{1,0:T(8,128)S(1)} %slice_select_fusion), channel_id=1, source_target_pairs={{0,1},{1,0},{2,3},{3,2},{4,5},{5,4},{6,7},{7,6},{8,9},{9,8},{10,11... | collective-permute-start | bytes 36872 | tf_op jit(solution)/shard_map/ppermute | solution.py:18
  3.9 0.6 %gram.2 = f32[576,128]{1,0:T(8,128)S(1)} custom-call(s32[1]{0:T(128)} %bitcast.1.side_ref.refs_0_, bf16[768,512]{1,0:T(8,128)(2,1)S(1)} %bitcast.22), custom_call_target="tpu_custom_call" | custom-call | flops 113246208 | bytes 294912 | tf_op jit(solution)/shard_map/gram/pallas_call | solution.py:88
  4.5 0.9 %collective-permute-done.1 = f32[576,128]{1,0:T(8,128)S(1)} collective-permute-done((f32[576,128]{1,0:T(8,128)S(1)}, f32[576,128]{1,0:T(8,128)S(1)}, u32[]{:S(2)}, u32[]{:S(2)}) %collective-permute-start.1) | collective-permute-done | bytes 294944 | tf_op jit(solution)/shard_map/ppermute | solution.py:18
  5.5 3.6 %collective-permute-start.4 = (f32[152,128]{1,0:T(8,128)S(1)}, f32[152,128]{1,0:T(8,128)S(1)}, u32[]{:S(2)}, u32[]{:S(2)}) collective-permute-start(f32[152,128]{1,0:T(8,128)S(1)} %pad_maximum_fusion.2), channel_id=1, source_target_pairs={{0,6},{1,25},{2,4},{3,27},{4,2},{5,29},{6,0},{7,31},{8,14},{9,17},... | collective-permute-start | bytes 233480 | tf_op jit(solution)/shard_map/ppermute | solution.py:26
  9.8 4.2 %collective-permute-done.3 = f32[144,128]{1,0:T(8,128)S(1)} collective-permute-done((f32[144,128]{1,0:T(8,128)S(1)}, f32[144,128]{1,0:T(8,128)S(1)}, u32[]{:S(2)}, u32[]{:S(2)}) %collective-permute-start.3) | collective-permute-done | bytes 73760 | tf_op jit(solution)/shard_map/ppermute | solution.py:26
  14.1 3.7 %collective-permute-start.6 = (f32[152,128]{1,0:T(8,128)S(1)}, f32[152,128]{1,0:T(8,128)S(1)}, u32[]{:S(2)}, u32[]{:S(2)}) collective-permute-start(f32[152,128]{1,0:T(8,128)S(1)} %get-tuple-element.39), channel_id=1, source_target_pairs={{0,24},{1,7},{2,26},{3,5},{4,28},{5,3},{6,30},{7,1},{8,16},{9,15},... | collective-permute-start | bytes 233480 | tf_op jit(solution)/shard_map/ppermute | solution.py:26
  17.7 0.8 %collective-permute-start.7 = (f32[144,128]{1,0:T(8,128)S(1)}, f32[144,128]{1,0:T(8,128)S(1)}, u32[]{:S(2)}, u32[]{:S(2)}) collective-permute-start(f32[144,128]{1,0:T(8,128)S(1)} %slice_add_fusion.2), channel_id=1, source_target_pairs={{0,16},{1,5},{2,18},{3,7},{4,20},{5,1},{6,22},{7,3},{8,24},{9,13},... | collective-permute-start | bytes 221192 | tf_op jit(solution)/shard_map/ppermute | solution.py:26
  18.5 1.9 %collective-permute-done.6 = f32[152,128]{1,0:T(8,128)S(1)} collective-permute-done((f32[152,128]{1,0:T(8,128)S(1)}, f32[152,128]{1,0:T(8,128)S(1)}, u32[]{:S(2)}, u32[]{:S(2)}) %collective-permute-start.6) | collective-permute-done | bytes 77856 | tf_op jit(solution)/shard_map/ppermute | solution.py:26
  20.4 1.8 %collective-permute-done.5 = f32[152,128]{1,0:T(8,128)S(1)} collective-permute-done((f32[152,128]{1,0:T(8,128)S(1)}, f32[152,128]{1,0:T(8,128)S(1)}, u32[]{:S(2)}, u32[]{:S(2)}) %collective-permute-start.5) | collective-permute-done | bytes 77856 | tf_op jit(solution)/shard_map/ppermute | solution.py:26
  22.4 0.6 %collective-permute-done.7 = f32[144,128]{1,0:T(8,128)S(1)} collective-permute-done((f32[144,128]{1,0:T(8,128)S(1)}, f32[144,128]{1,0:T(8,128)S(1)}, u32[]{:S(2)}, u32[]{:S(2)}) %collective-permute-start.7) | collective-permute-done | bytes 73760 | tf_op jit(solution)/shard_map/ppermute | solution.py:26
  23.0 1.5 %collective-permute-start.10 = (f32[152,128]{1,0:T(8,128)S(1)}, f32[152,128]{1,0:T(8,128)S(1)}, u32[]{:S(2)}, u32[]{:S(2)}) collective-permute-start(f32[152,128]{1,0:T(8,128)S(1)} %pad_maximum_fusion.5), channel_id=1, source_target_pairs={{0,6},{1,25},{2,4},{3,27},{4,2},{5,29},{6,0},{7,31},{8,14},{9,17},... | collective-permute-start | bytes 233480 | tf_op jit(solution)/shard_map/ppermute | solution.py:26
  24.5 1.5 %collective-permute-start.9 = (f32[152,128]{1,0:T(8,128)S(1)}, f32[152,128]{1,0:T(8,128)S(1)}, u32[]{:S(2)}, u32[]{:S(2)}) collective-permute-start(f32[152,128]{1,0:T(8,128)S(1)} %pad_maximum_fusion.5), channel_id=1, source_target_pairs={{0,4},{1,17},{2,6},{3,19},{4,0},{5,21},{6,2},{7,23},{8,12},{9,25},... | collective-permute-start | bytes 233480 | tf_op jit(solution)/shard_map/ppermute | solution.py:26
  26.0 0.5 collective-permute-start.8
  26.6 1.8 %collective-permute-done.10 = f32[152,128]{1,0:T(8,128)S(1)} collective-permute-done((f32[152,128]{1,0:T(8,128)S(1)}, f32[152,128]{1,0:T(8,128)S(1)}, u32[]{:S(2)}, u32[]{:S(2)}) %collective-permute-start.10) | collective-permute-done | bytes 77856 | tf_op jit(solution)/shard_map/ppermute | solution.py:26
  28.4 0.8 %collective-permute-done.9 = f32[152,128]{1,0:T(8,128)S(1)} collective-permute-done((f32[152,128]{1,0:T(8,128)S(1)}, f32[152,128]{1,0:T(8,128)S(1)}, u32[]{:S(2)}, u32[]{:S(2)}) %collective-permute-start.9) | collective-permute-done | bytes 77856 | tf_op jit(solution)/shard_map/ppermute | solution.py:26
  29.2 1.2 %collective-permute-done.8 = f32[152,128]{1,0:T(8,128)S(1)} collective-permute-done((f32[152,128]{1,0:T(8,128)S(1)}, f32[152,128]{1,0:T(8,128)S(1)}, u32[]{:S(2)}, u32[]{:S(2)}) %collective-permute-start.8) | collective-permute-done | bytes 77856 | tf_op jit(solution)/shard_map/ppermute | solution.py:26
  30.6 2.1 %collective-permute-start.11 = (f32[8,128]{1,0:T(8,128)S(1)}, f32[8,128]{1,0:T(8,128)S(1)}, u32[]{:S(2)}, u32[]{:S(2)}) collective-permute-start(f32[8,128]{1,0:T(8,128)S(1)} %slice_add_fusion.5), channel_id=1, source_target_pairs={{0,8},{1,3},{2,10},{3,1},{4,12},{5,7},{6,14},{7,5},{8,0},{9,11},{1... | collective-permute-start | bytes 12296 | tf_op jit(solution)/shard_map/ppermute | solution.py:26
  32.7 1.6 %collective-permute-done.11 = f32[8,128]{1,0:T(8,128)S(1)} collective-permute-done((f32[8,128]{1,0:T(8,128)S(1)}, f32[8,128]{1,0:T(8,128)S(1)}, u32[]{:S(2)}, u32[]{:S(2)}) %collective-permute-start.11) | collective-permute-done | bytes 4128 | tf_op jit(solution)/shard_map/ppermute | solution.py:26
  34.2 1.7 %collective-permute-start.12 = (f32[8,128]{1,0:T(8,128)S(1)}, f32[8,128]{1,0:T(8,128)S(1)}, u32[]{:S(2)}, u32[]{:S(2)}) collective-permute-start(f32[8,128]{1,0:T(8,128)S(1)} %add.75), channel_id=1, source_target_pairs={{0,16},{1,5},{2,18},{3,7},{4,20},{5,1},{6,22},{7,3},{8,24},{9,13},... | collective-permute-start | bytes 12296 | tf_op jit(solution)/shard_map/ppermute | solution.py:26
  35.9 2.8 %collective-permute-done.12 = f32[8,128]{1,0:T(8,128)S(1)} collective-permute-done((f32[8,128]{1,0:T(8,128)S(1)}, f32[8,128]{1,0:T(8,128)S(1)}, u32[]{:S(2)}, u32[]{:S(2)}) %collective-permute-start.12) | collective-permute-done | bytes 4128 | tf_op jit(solution)/shard_map/ppermute | solution.py:26
  38.8 7.3 %early.1 = (f32[512,512]{1,0:T(8,128)S(1)}, f32[256,512]{1,0:T(8,128)S(1)}) custom-call(s32[1]{0:T(128)} %bitcast.1.side_ref.refs_0_, s32[1]{0:T(128)} %bitcast.9.refs_1_, s32[1]{0:T(128)} %bitcast.10.refs_2_, f32[576,128]{1,0:T(8,128)S(1)} %pad_maximum_fusion.refs_3_, f32[576,128]{1,0:T(8,128)S(1)} %collective-permute-done.13.refs_4_), custom_call_target="tpu_custom_call" | custom-call | flops 2147483648 | bytes 2097152 | tf_op jit(solution)/shard_map/early/pallas_call | solution.py:376
  46.2 8.4 %late.1 = (f32[512,512]{1,0:T(8,128)S(1)}, bf16[768,512]{1,0:T(8,128)(2,1)}, f32[513,513]{1,0:T(8,128)}) custom-call(f32[512,512]{1,0:T(8,128)S(1)} %get-tuple-element.20.early_ref, f32[256,512]{1,0:T(8,128)S(1)} %get-tuple-element.21.early_upper_ref, bf16[768,512]{1,0:T(8,128)(2,1)S(1)} %bitcast.24), custom_call_target="tpu_custom_call" | custom-call | flops 2147483648 | bytes 2097152 | tf_op jit(solution)/shard_map/late/pallas_call | solution.py:433
  54.6 1.1 %finish.1 = (f32[1,768]{1,0:T(1,128)}, f32[513,513]{1,0:T(8,128)}) custom-call(f32[512,512]{1,0:T(8,128)S(1)} %get-tuple-element.23.refs_0_, f32[8,128]{1,0:T(8,128)S(1)} %add.77.refs_1_, f32[6,128]{1,0:T(8,128)S(1)} %get-tuple-element.25.refs_2_, bf16[768,512]{1,0:T(8,128)(2,1)S(1)} %bitcast.25, ...), custom_call_target="tpu_custom_call", output_to_operand_aliasing={{1}: (4, {})} | custom-call | flops 16777216 | bytes 1048576 | tf_op jit(solution)/shard_map/finish/pallas_call | solution.py:489
  (36 shorter events, 1.8 us)
Async XLA Ops:
  0.6 2.7 %copy-start = (bf16[3,1,2,128,512]{4,3,2,1,0:T(8,128)(2,1)S(1)}, bf16[3,1,2,128,512]{4,3,2,1,0:T(8,128)(2,1)}, u32[]{:S(2)}) copy-start(bf16[3,1,2,128,512]{4,3,2,1,0:T(8,128)(2,1)} %param.4) | copy-start | bytes 2359300
  2.8 1.7 %collective-permute-start = (f32[24,128]{1,0:T(8,128)S(1)}, f32[24,128]{1,0:T(8,128)S(1)}, u32[]{:S(2)}, u32[]{:S(2)}) collective-permute-start(f32[24,128]{1,0:T(8,128)S(1)} %slice_select_fusion), channel_id=1, source_target_pairs={{0,1},{1,0},{2,3},{3,2},{4,5},{5,4},{6,7},{7,6},{8,9},{9,8},{10,11... | collective-permute-start | bytes 36872 | tf_op jit(solution)/shard_map/ppermute | solution.py:18
  3.8 1.6 %collective-permute-start.1 = (f32[576,128]{1,0:T(8,128)S(1)}, f32[576,128]{1,0:T(8,128)S(1)}, u32[]{:S(2)}, u32[]{:S(2)}) collective-permute-start(f32[576,128]{1,0:T(8,128)S(1)} %gram.3), channel_id=1, source_target_pairs={{0,1},{1,0},{2,3},{3,2},{4,5},{5,4},{6,7},{7,6},{8,9},{9,8},{10,11... | collective-permute-start | bytes 884744 | tf_op jit(solution)/shard_map/ppermute | solution.py:18
  5.5 8.5 %collective-permute-start.4 = (f32[152,128]{1,0:T(8,128)S(1)}, f32[152,128]{1,0:T(8,128)S(1)}, u32[]{:S(2)}, u32[]{:S(2)}) collective-permute-start(f32[152,128]{1,0:T(8,128)S(1)} %pad_maximum_fusion.2), channel_id=1, source_target_pairs={{0,6},{1,25},{2,4},{3,27},{4,2},{5,29},{6,0},{7,31},{8,14},{9,17},... | collective-permute-start | bytes 233480 | tf_op jit(solution)/shard_map/ppermute | solution.py:26
  9.1 4.9 %collective-permute-start.2 = (f32[152,128]{1,0:T(8,128)S(1)}, f32[152,128]{1,0:T(8,128)S(1)}, u32[]{:S(2)}, u32[]{:S(2)}) collective-permute-start(f32[152,128]{1,0:T(8,128)S(1)} %pad_maximum_fusion.1), channel_id=1, source_target_pairs={{0,2},{1,9},{2,0},{3,11},{4,6},{5,13},{6,4},{7,15},{8,10},{9,1},{1... | collective-permute-start | bytes 233480 | tf_op jit(solution)/shard_map/ppermute | solution.py:26
  9.6 4.4 %collective-permute-start.3 = (f32[144,128]{1,0:T(8,128)S(1)}, f32[144,128]{1,0:T(8,128)S(1)}, u32[]{:S(2)}, u32[]{:S(2)}) collective-permute-start(f32[144,128]{1,0:T(8,128)S(1)} %get-tuple-element.34), channel_id=1, source_target_pairs={{0,4},{1,17},{2,6},{3,19},{4,0},{5,21},{6,2},{7,23},{8,12},{9,25},... | collective-permute-start | bytes 221192 | tf_op jit(solution)/shard_map/ppermute | solution.py:26
  14.1 6.3 %collective-permute-start.6 = (f32[152,128]{1,0:T(8,128)S(1)}, f32[152,128]{1,0:T(8,128)S(1)}, u32[]{:S(2)}, u32[]{:S(2)}) collective-permute-start(f32[152,128]{1,0:T(8,128)S(1)} %get-tuple-element.39), channel_id=1, source_target_pairs={{0,24},{1,7},{2,26},{3,5},{4,28},{5,3},{6,30},{7,1},{8,16},{9,15},... | collective-permute-start | bytes 233480 | tf_op jit(solution)/shard_map/ppermute | solution.py:26
  17.7 4.4 %collective-permute-start.5 = (f32[152,128]{1,0:T(8,128)S(1)}, f32[152,128]{1,0:T(8,128)S(1)}, u32[]{:S(2)}, u32[]{:S(2)}) collective-permute-start(f32[152,128]{1,0:T(8,128)S(1)} %get-tuple-element.40), channel_id=1, source_target_pairs={{0,8},{1,3},{2,10},{3,1},{4,12},{5,7},{6,14},{7,5},{8,0},{9,11},{1... | collective-permute-start | bytes 233480 | tf_op jit(solution)/shard_map/ppermute | solution.py:26
  17.7 5.3 %collective-permute-start.7 = (f32[144,128]{1,0:T(8,128)S(1)}, f32[144,128]{1,0:T(8,128)S(1)}, u32[]{:S(2)}, u32[]{:S(2)}) collective-permute-start(f32[144,128]{1,0:T(8,128)S(1)} %slice_add_fusion.2), channel_id=1, source_target_pairs={{0,16},{1,5},{2,18},{3,7},{4,20},{5,1},{6,22},{7,3},{8,24},{9,13},... | collective-permute-start | bytes 221192 | tf_op jit(solution)/shard_map/ppermute | solution.py:26
  23.0 5.4 %collective-permute-start.10 = (f32[152,128]{1,0:T(8,128)S(1)}, f32[152,128]{1,0:T(8,128)S(1)}, u32[]{:S(2)}, u32[]{:S(2)}) collective-permute-start(f32[152,128]{1,0:T(8,128)S(1)} %pad_maximum_fusion.5), channel_id=1, source_target_pairs={{0,6},{1,25},{2,4},{3,27},{4,2},{5,29},{6,0},{7,31},{8,14},{9,17},... | collective-permute-start | bytes 233480 | tf_op jit(solution)/shard_map/ppermute | solution.py:26
  24.5 4.7 %collective-permute-start.9 = (f32[152,128]{1,0:T(8,128)S(1)}, f32[152,128]{1,0:T(8,128)S(1)}, u32[]{:S(2)}, u32[]{:S(2)}) collective-permute-start(f32[152,128]{1,0:T(8,128)S(1)} %pad_maximum_fusion.5), channel_id=1, source_target_pairs={{0,4},{1,17},{2,6},{3,19},{4,0},{5,21},{6,2},{7,23},{8,12},{9,25},... | collective-permute-start | bytes 233480 | tf_op jit(solution)/shard_map/ppermute | solution.py:26
  26.0 4.4 %collective-permute-start.8 = (f32[152,128]{1,0:T(8,128)S(1)}, f32[152,128]{1,0:T(8,128)S(1)}, u32[]{:S(2)}, u32[]{:S(2)}) collective-permute-start(f32[152,128]{1,0:T(8,128)S(1)} %pad_maximum_fusion.5), channel_id=1, source_target_pairs={{0,2},{1,9},{2,0},{3,11},{4,6},{5,13},{6,4},{7,15},{8,10},{9,1},{1... | collective-permute-start | bytes 233480 | tf_op jit(solution)/shard_map/ppermute | solution.py:26
  30.5 8.3 %collective-permute-start.13 = (f32[576,128]{1,0:T(8,128)S(1)}, f32[576,128]{1,0:T(8,128)S(1)}, u32[]{:S(2)}, u32[]{:S(2)}) collective-permute-start(f32[576,128]{1,0:T(8,128)S(1)} %pad_maximum_fusion.refs_3_), channel_id=1, source_target_pairs={{0,1},{1,0},{2,3},{3,2},{4,5},{5,4},{6,7},{7,6},{8,9},{9,8},{10,11... | collective-permute-start | bytes 884744 | tf_op jit(solution)/shard_map/ppermute | solution.py:18
  30.6 3.7 %collective-permute-start.11 = (f32[8,128]{1,0:T(8,128)S(1)}, f32[8,128]{1,0:T(8,128)S(1)}, u32[]{:S(2)}, u32[]{:S(2)}) collective-permute-start(f32[8,128]{1,0:T(8,128)S(1)} %slice_add_fusion.5), channel_id=1, source_target_pairs={{0,8},{1,3},{2,10},{3,1},{4,12},{5,7},{6,14},{7,5},{8,0},{9,11},{1... | collective-permute-start | bytes 12296 | tf_op jit(solution)/shard_map/ppermute | solution.py:26
  34.2 4.5 %collective-permute-start.12 = (f32[8,128]{1,0:T(8,128)S(1)}, f32[8,128]{1,0:T(8,128)S(1)}, u32[]{:S(2)}, u32[]{:S(2)}) collective-permute-start(f32[8,128]{1,0:T(8,128)S(1)} %add.75), channel_id=1, source_target_pairs={{0,16},{1,5},{2,18},{3,7},{4,20},{5,1},{6,22},{7,3},{8,24},{9,13},... | collective-permute-start | bytes 12296 | tf_op jit(solution)/shard_map/ppermute | solution.py:26
  46.1 8.5 %collective-permute-start.14 = (f32[8,128]{1,0:T(8,128)S(1)}, f32[8,128]{1,0:T(8,128)S(1)}, u32[]{:S(2)}, u32[]{:S(2)}) collective-permute-start(f32[8,128]{1,0:T(8,128)S(1)} %add.76), channel_id=1, source_target_pairs={{0,1},{1,0},{2,3},{3,2},{4,5},{5,4},{6,7},{7,6},{8,9},{9,8},{10,11... | collective-permute-start | bytes 12296 | tf_op jit(solution)/shard_map/ppermute | solution.py:18
